TPU v7x, 1024 devices: a whole 8x8x8 slice. The times are simulated.
1024 devices in a mesh: prow: 32 (over x, z_lo), pcol: 16 (over y, z_hi), layer: 2 (over core).
Axes of the slice: x: 8, y: 8, z: 8 (z_hi: 2, z_lo: 4; z = z_hi * 4 + z_lo), core: 2. Of those that a mesh axis runs over, the one named last changes fastest.
Arguments:
- p_vals: bfloat16 [512, 64, 1536], P(('prow', 'pcol'), None, 'layer'), may hold values from -2 to 2
- p_cols: int32 [512, 24], P(('prow', 'pcol'), 'layer'), may hold values from 0 to 511, as said below
- c_cols: int32 [512, 16, 6], P('prow', 'pcol'), may hold values from 0 to 511, as said below
Outputs:
- c_vals: bfloat16 [512, 16, 64, 384], P('prow', 'pcol', None, 'layer')
Inputs may be any that keep to these rules, and one draw needn't show every extreme that they name: `p_cols`: the first 12 block columns of every row are even and the rest odd; within a row the 24 block columns are distinct. `c_cols`: for row i and group c the 6 columns are distinct and each column j has (j) % (16) == c.
All inputs are finite; a program needn't handle non-finite values.
Results may differ from a plain program's by a relative error of at most 0.002.
Values may be sent and summed in bfloat16 or wider, within the bound.
A program may use at most 32 MiB of HBM per device.

v0:
```python
import jax
import jax.numpy as jnp
from jax import lax
from jax.sharding import PartitionSpec as P


def tile_product(row_vals, row_cols, col_vals, col_cols, targets):

    def one_row(row_data):
        row_block, row_index, wanted = row_data
        picked = jnp.take(col_vals, wanted, axis=0)
        picked_cols = jnp.take(col_cols, wanted, axis=0)
        out_count = wanted.shape[0]
        slot_count = row_index.shape[0]
        block_edge = row_block.shape[0]
        matched = (row_index[None, :, None] == picked_cols[:, None, :]).astype(jnp.bfloat16)
        blocks = picked.reshape(out_count, block_edge, slot_count, block_edge)
        chosen = jnp.einsum(
            "oab,oybz->oyaz", matched, blocks, preferred_element_type=jnp.float32
        ).astype(jnp.bfloat16)
        chosen = chosen.reshape(out_count, block_edge, slot_count * block_edge)
        product = jnp.einsum("xk,oyk->xoy", row_block, chosen, preferred_element_type=jnp.float32)
        return product.reshape(block_edge, out_count * block_edge)

    return lax.map(one_row, (row_vals, row_cols, targets))


def per_device(p_vals, p_cols, c_cols):
    shard_rows = p_vals.shape[0]
    grid_width = lax.axis_size("pcol") * shard_rows
    wanted_cols = c_cols[:, 0, :]
    targets = wanted_cols // grid_width * shard_rows + wanted_cols % shard_rows
    row_vals, row_cols = (
        lax.all_gather(p_vals, "pcol", axis=0, tiled=True),
        lax.all_gather(p_cols, "pcol", axis=0, tiled=True),
    )
    col_vals, col_cols = (
        lax.all_gather(p_vals, "prow", axis=0, tiled=True),
        lax.all_gather(p_cols, "prow", axis=0, tiled=True),
    )
    partial_value = tile_product(row_vals, row_cols, col_vals, col_cols, targets)
    own_share = lax.psum_scatter(partial_value, "layer", scatter_dimension=2, tiled=True)
    result = own_share.astype(jnp.bfloat16)
    return result[:, None]


def solution(mesh):
    return jax.shard_map(
        per_device,
        mesh=mesh,
        in_specs=(
            P(("prow", "pcol"), None, "layer"),
            P(("prow", "pcol"), "layer"),
            P("prow", "pcol", None),
        ),
        out_specs=P("prow", "pcol", None, "layer"),
        check_vma=False,
    )
```

profile of v0, /device:TPU:1, one launch (start us, length us, event | category | flops | bytes accessed | tf_op | source)
XLA Modules:
  0.0 445.9 jit_solution(6172893762584280432)
XLA Ops:
  8.8 55.0 %all-gather = s32[16,1,12]{2,1,0:T(1,128)S(1)} all-gather(s32[1,1,12]{2,1,0:T(1,128)} %bitcast.71), channel_id=1, replica_groups=mesh['prow'=32,'pcol'=16,'layer'=2] {'pcol'}, dimensions={0}, use_global_device_ids=true | all-gather | bytes 816 | tf_op jit(solution)/shard_map/all_gather | solution.py:35
  63.9 68.3 %all-gather.1 = s32[32,1,12]{2,1,0:T(1,128)S(1)} all-gather(s32[1,1,12]{2,1,0:T(1,128)} %bitcast.72), channel_id=1, replica_groups=mesh['prow'=32,'pcol'=16,'layer'=2] {'prow'}, dimensions={0}, use_global_device_ids=true | all-gather | bytes 1584 | tf_op jit(solution)/shard_map/all_gather | solution.py:39
  132.2 134.5 %all-gather.7.cloned.1.call-done = bf16[32,64,768]{2,1,0:T(8,128)(2,1)} async-done(((bf16[1,64,768]{2,1,0:T(8,128)(2,1)}), bf16[32,64,768]{2,1,0:T(8,128)(2,1)}) %all-gather.7.cloned.1.call-update) | async-done | bytes 3145744 | tf_op jit(solution)/shard_map/all_gather | solution.py:38
  266.7 121.1 %while.10 = (s32[]{:T(128)}, f32[16,64,384]{2,1,0:T(8,128)}, bf16[16,64,768]{2,1,0:T(8,128)(2,1)}, s32[16,6]{1,0:T(8,128)S(1)}, bf16[32,64,768]{2,1,0:T(8,128)(2...) while((s32[]{:T(128)}, f32[16,64,384]{2,1,0:T(8,128)}, bf16[16,64,768]{2,1,0:T(8,128)(2,1)}, ...), condition=%wide.region_1.2_spmd, body=%wide.region_0.1_spmd.sunk | while | flops 45418464 | bytes 5511987 | solution.py:25
  267.4 2.5 gather_fusion
  269.8 1.0 gather.19
  271.5 0.9 dot_general.11
  272.4 1.8 fusion.36
  274.9 2.5 gather_fusion
  277.4 1.0 gather.19
  279.1 0.9 dot_general.11
  280.0 1.8 fusion.36
  282.5 2.5 gather_fusion
  285.0 1.0 gather.19
  286.6 0.9 dot_general.11
  287.6 1.8 fusion.36
  290.1 2.5 gather_fusion
  292.5 1.0 gather.19
  294.2 0.9 dot_general.11
  295.1 1.8 fusion.36
  297.6 2.5 gather_fusion
  300.1 1.0 gather.19
  301.8 0.9 dot_general.11
  302.7 1.8 fusion.36
  305.2 2.5 gather_fusion
  307.7 1.0 gather.19
  310.3 1.8 fusion.36
  312.8 2.5 gather_fusion
  315.2 1.0 gather.19
  316.9 0.9 dot_general.11
  317.8 1.8 fusion.36
  320.3 2.5 gather_fusion
  322.8 1.0 gather.19
  325.4 1.9 fusion.36
  327.9 2.5 gather_fusion
  330.4 1.0 gather.19
  333.0 1.8 fusion.36
  335.5 2.5 gather_fusion
  338.0 1.0 gather.19
  340.5 1.8 fusion.36
  343.1 2.5 gather_fusion
  345.5 1.0 gather.19
  347.2 0.9 dot_general.11
  348.1 1.8 fusion.36
  350.6 2.5 gather_fusion
  353.1 1.0 gather.19
  355.7 1.8 fusion.36
  358.2 2.5 gather_fusion
  360.7 1.0 gather.19
  363.2 1.8 fusion.36
  365.8 2.5 gather_fusion
  368.2 1.0 gather.19
  370.8 1.8 fusion.36
  373.3 2.5 gather_fusion
  375.8 1.0 gather.19
  378.4 1.8 fusion.36
  380.9 2.5 gather_fusion
  383.4 1.0 gather.19
  385.9 1.8 fusion.36
  387.8 2.4 copy.9
  390.2 1.8 reshape.82
  392.0 44.2 %reduce-scatter.4.cloned.1.call-done = f32[192,1024]{1,0:T(8,128)} async-done(((f32[384,1024]{1,0:T(8,128)}), f32[192,1024]{1,0:T(8,128)}) %reduce-scatter.4.cloned.1.call-update) | async-done | bytes 786448
  436.2 1.7 reshape.83
  437.9 1.5 copy.10
  (131 shorter events, 31.2 us)
Async XLA Ops:
  6.5 125.6 %all-gather.5.cloned.1.call-start = ((), (), s32[]{:S(2)}) async-start(), calls=%async_computation.1 | async-start | bytes 1671168 | tf_op jit(solution)/shard_map/all_gather | solution.py:34
  7.3 259.4 %all-gather.7.cloned.1.call-start = ((), (), s32[]{:S(2)}) async-start(), calls=%async_computation.2 | async-start | bytes 3244032 | tf_op jit(solution)/shard_map/all_gather | solution.py:38
  8.0 428.2 %reduce-scatter.4.cloned.1.call-start = ((), (), s32[]{:S(2)}) async-start(), calls=%async_computation.3 | async-start | bytes 2359296
Sparse Core Ops, SparseCore 0:
  11.7 114.9 all-gather.4
  129.4 137.2 all-gather.6
  392.2 43.9 reduce-scatter.3
where the time goes:
time: 447 us; the launch traced here: 446 us
  waiting for transfers between devices  180 us (40%)
  blocking collectives  123 us (28%)
  local copies, waits for them, and re-layouts  86.6 us (19%)
  matrix products  39.5 us (9%)
  between operations  13.1 us (3%)
    all_gather x1, waiting for transfers between devices, per_device(): lax.all_gather(p_vals, 'prow', axis=0, tiled=True)  135 us
    all_gather x1, blocking collectives, per_device(): lax.all_gather(p_cols, 'prow', axis=0, tiled=True)  68.3 us
    gather x32, local copies, waits for them, and re-layouts, one_row(): picked = jnp.take(col_vals, wanted, axis=0)  55.5 us
    all_gather x1, blocking collectives, per_device(): lax.all_gather(p_cols, 'pcol', axis=0, tiled=True)  55 us
    unnamed x4, waiting for transfers between devices  45.6 us
    dot_general x16, matrix products, one_row(): jnp.einsum('xk,oyk->xoy', row_block, chosen, preferred_element_type=jnp.f...  29.5 us
    dot_general x16, local copies, waits for them, and re-layouts, one_row(): jnp.einsum('xk,oyk->xoy', row_block, chosen, preferred_element_type=jnp.f...  14.6 us
    dot_general x16, matrix products, one_row(): jnp.einsum('oab,oybz->oyaz', matched, blocks, preferred_element_type=jnp....  9.94 us
  transfers between devices with their start and end apart: 3, of which 2 were waited for; matrix products, arithmetic and copies ran while one was open for 0% of the time, Pallas kernels for 0%

commit v1 on v0

v1 whole, which is shorter than its diff:
```python
import jax
import jax.numpy as jnp
from jax import lax
from jax.experimental import pallas as pl
from jax.experimental.pallas import tpu as pltpu
from jax.sharding import PartitionSpec as P

MESH = pl.DeviceIdType.MESH
NX, NZ, NY, NH = 8, 4, 8, 2
COLS, ROWS = NX * NZ, NY * NH
LANES = 128


def gather_kernel(vals, cols, colv, colc, rowv, rowc, a_send, a_recv, b_send, b_recv, own_sem):
    me_p = lax.axis_index("prow")
    me_q = lax.axis_index("pcol")
    x, z = me_p // NZ, me_p % NZ
    y, h = me_q // NH, me_q % NH

    def on_p(dx, dz):
        return (x + dx + NX) % NX * NZ + (z + dz + NZ) % NZ

    def on_q(dy, dh):
        return (y + dy + NY) % NY * NH + (h + dh) % NH

    barrier = pltpu.get_barrier_semaphore()
    partners = [{"prow": on_p(0, k)} for k in range(1, NZ)]
    partners += [{"prow": on_p(1, 0)}, {"prow": on_p(-1, 0)}]
    partners += [{"pcol": on_q(0, 1)}, {"pcol": on_q(1, 0)}, {"pcol": on_q(-1, 0)}]
    for who in partners:
        pl.semaphore_signal(barrier, inc=1, device_id=who, device_id_type=MESH)
    pl.semaphore_wait(barrier, len(partners))

    def copies(dst_v, dst_c, slot, own, sends, recvs, sid, who):
        src_v = vals.at[0] if own else dst_v.at[slot]
        src_c = cols.at[0] if own else dst_c.at[slot]
        return [
            pltpu.make_async_remote_copy(
                src_ref=src,
                dst_ref=dst.at[slot],
                send_sem=sends.at[k, sid],
                recv_sem=recvs.at[k, sid],
                device_id=who,
                device_id_type=MESH,
            )
            for k, (src, dst) in enumerate(((src_c, dst_c), (src_v, dst_v)))
        ]

    sent = []

    def send_a(slot, own, sid, who):
        for c in copies(colv, colc, slot, own, a_send, a_recv, sid, {"prow": who}):
            c.start()
            sent.append(c)

    def send_b(slot, own, sid, who):
        for c in copies(rowv, rowc, slot, own, b_send, b_recv, sid, {"pcol": who}):
            c.start()
            sent.append(c)

    def recv_a(slot, sid):
        for c in copies(colv, colc, slot, False, a_send, a_recv, sid, {"prow": on_p(1, 0)}):
            c.wait_recv()

    def recv_b(slot, sid):
        for c in copies(rowv, rowc, slot, False, b_send, b_recv, sid, {"pcol": on_q(1, 0)}):
            c.wait_recv()

    def a_right(d, q):
        return NZ + (d - 1) * NZ + q

    def a_left(d, q):
        return NZ + (NX // 2) * NZ + (d - 1) * NZ + q

    def b_right(d, p):
        return 1 + (d - 1) * NH + p

    def b_left(d, p):
        return 1 + (NY // 2) * NH + (d - 1) * NH + p

    def forward_a(slot, own, d, q):
        if d < NX // 2 - 1 or q < NZ // 2:
            send_a(slot, own, a_right(d + 1, q), on_p(1, 0))

    def forward_a_left(slot, own, d, q):
        if d < NX // 2 - 1 or q >= NZ // 2:
            send_a(slot, own, a_left(d + 1, q), on_p(-1, 0))

    def forward_b(slot, own, d, p):
        if d < NY // 2 - 1 or p == 0:
            send_b(slot, own, b_right(d + 1, p), on_q(1, 0))

    def forward_b_left(slot, own, d, p):
        if d < NY // 2 - 1 or p == 1:
            send_b(slot, own, b_left(d + 1, p), on_q(-1, 0))

    forward_a(me_p, True, 0, 0)
    forward_a_left(me_p, True, 0, 0)
    forward_b(me_q, True, 0, 0)
    forward_b_left(me_q, True, 0, 0)
    for k in range(1, NZ):
        send_a(me_p, True, k, on_p(0, k))
    send_b(me_q, True, 0, on_q(0, 1))
    own_copies = [
        pltpu.make_async_copy(vals.at[0], colv.at[me_p], own_sem.at[0]),
        pltpu.make_async_copy(cols.at[0], colc.at[me_p], own_sem.at[1]),
        pltpu.make_async_copy(vals.at[0], rowv.at[me_q], own_sem.at[2]),
        pltpu.make_async_copy(cols.at[0], rowc.at[me_q], own_sem.at[3]),
    ]
    for c in own_copies:
        c.start()

    for q in range(1, NZ):
        recv_a(on_p(0, -q), q)
        forward_a(on_p(0, -q), False, 0, q)
        forward_a_left(on_p(0, -q), False, 0, q)
    recv_b(on_q(0, 1), 0)
    forward_b(on_q(0, 1), False, 0, 1)
    forward_b_left(on_q(0, 1), False, 0, 1)

    for d in range(1, NX // 2 + 1):
        last = d == NX // 2
        for q in range(NZ):
            if not last or q < NZ // 2:
                recv_a(on_p(-d, -q), a_right(d, q))
                if not last:
                    forward_a(on_p(-d, -q), False, d, q)
            if not last or q >= NZ // 2:
                recv_a(on_p(d, -q), a_left(d, q))
                if not last:
                    forward_a_left(on_p(d, -q), False, d, q)
            if q % 2 == 1:
                p = q // 2
                if not last or p == 0:
                    recv_b(on_q(-d, p), b_right(d, p))
                    if not last:
                        forward_b(on_q(-d, p), False, d, p)
                if not last or p == 1:
                    recv_b(on_q(d, p), b_left(d, p))
                    if not last:
                        forward_b_left(on_q(d, p), False, d, p)
    for c in own_copies:
        c.wait()
    for c in sent:
        c.wait_send()


def gather(vals, cols):
    n_a = NZ + NX * NZ
    n_b = 1 + NY * NH
    dma = pltpu.SemaphoreType.DMA
    shape = vals.shape[1:]
    return pl.pallas_call(
        gather_kernel,
        name="gather_both",
        out_shape=(
            jax.ShapeDtypeStruct((COLS,) + shape, vals.dtype),
            jax.ShapeDtypeStruct((COLS, 1, LANES), jnp.int32),
            jax.ShapeDtypeStruct((ROWS,) + shape, vals.dtype),
            jax.ShapeDtypeStruct((ROWS, 1, LANES), jnp.int32),
        ),
        in_specs=[pl.BlockSpec(memory_space=pltpu.VMEM)] * 2,
        out_specs=[pl.BlockSpec(memory_space=pl.ANY)] * 4,
        scratch_shapes=[dma((2, n_a)), dma((2, n_a)), dma((2, n_b)), dma((2, n_b)), dma((4,))],
        compiler_params=pltpu.CompilerParams(collective_id=0, has_side_effects=True),
    )(vals, cols)


def product_kernel(
    picks, rowv, colv, out, rows, stage, twice, chosen, own, send, recv, row_sem, col_sem, send_sem, recv_sem
):
    n_rows, edge, width = rows.shape
    slots = width // edge
    per_copy = COLS // col_sem.shape[0]
    groups = col_sem.shape[0]
    half = own.shape[2] // edge
    me = lax.axis_index("layer")
    other = {"layer": 1 - me}

    row_copy = pltpu.make_async_copy(rowv, rows, row_sem)
    col_copies = [
        pltpu.make_async_copy(
            colv.at[pl.ds(g * per_copy, per_copy)], stage.at[pl.ds(g * per_copy, per_copy)], col_sem.at[g]
        )
        for g in range(groups)
    ]
    for c in col_copies:
        c.start()
    row_copy.start()
    barrier = pltpu.get_barrier_semaphore()
    pl.semaphore_signal(barrier, inc=1, device_id=other, device_id_type=MESH)
    low = lax.broadcasted_iota(jnp.int32, (edge, LANES), 1) < edge
    twice[COLS * slots] = jnp.zeros((edge, LANES), twice.dtype)
    for g in range(groups):
        col_copies[g].wait()

        def spread(j, carry):
            for b in range(slots // 2):
                pair = stage[j, :, b * LANES : (b + 1) * LANES]
                turned = jnp.concatenate([pair[:, edge:], pair[:, :edge]], axis=1)
                twice[j * slots + 2 * b] = jnp.where(low, pair, turned)
                twice[j * slots + 2 * b + 1] = jnp.where(low, turned, pair)
            return carry

        lax.fori_loop(g * per_copy, (g + 1) * per_copy, spread, 0)
    row_copy.wait()
    pl.semaphore_wait(barrier, 1)

    def swap(i):
        return pltpu.make_async_remote_copy(
            src_ref=send.at[i],
            dst_ref=recv.at[i],
            send_sem=send_sem.at[i],
            recv_sem=recv_sem.at[i],
            device_id=other,
            device_id_type=MESH,
        )

    def one_row(i, carry):
        a = rows[i]
        for side, target in ((1, send), (0, own)):
            for o in range(half):
                for p in range(slots // 2):
                    at = (side * half + o) * slots + 2 * p
                    first = twice[picks[i, at]]
                    second = twice[picks[i, at + 1]]
                    chosen[side, o * edge : (o + 1) * edge, p * LANES : (p + 1) * LANES] = jnp.where(
                        low, first, second
                    )
            target[i] = lax.dot_general(
                a, chosen[side], (((1,), (1,)), ((), ())), preferred_element_type=jnp.float32
            )
            if side == 1:

                @pl.when(i > 0)
                def _():
                    swap(i - 1).start()

        return carry

    lax.fori_loop(0, n_rows, one_row, 0)
    swap(n_rows - 1).start()

    def finish(i, carry):
        swap(i).wait_recv()
        out[i, 0] = (own[i] + recv[i]).astype(out.dtype)
        return carry

    lax.fori_loop(0, n_rows, finish, 0)

    def drain(i, carry):
        swap(i).wait_send()
        return carry

    lax.fori_loop(0, n_rows, drain, 0)


def product(picks, rowv, colv, half):
    n_rows, edge, width = rowv.shape
    slots = width // edge
    groups = 8
    dma = pltpu.SemaphoreType.DMA
    share = (n_rows, edge, half * edge)
    return pl.pallas_call(
        product_kernel,
        name="pick_multiply_swap",
        out_shape=jax.ShapeDtypeStruct((n_rows, 1, edge, half * edge), rowv.dtype),
        in_specs=[
            pl.BlockSpec(memory_space=pltpu.SMEM),
            pl.BlockSpec(memory_space=pl.ANY),
            pl.BlockSpec(memory_space=pl.ANY),
        ],
        out_specs=pl.BlockSpec(memory_space=pltpu.VMEM),
        scratch_shapes=[
            pltpu.VMEM((n_rows, edge, width), rowv.dtype),
            pltpu.VMEM((COLS, edge, width), rowv.dtype),
            pltpu.VMEM((COLS * slots + 1, edge, LANES), rowv.dtype),
            pltpu.VMEM((2, half * edge, width), rowv.dtype),
            pltpu.VMEM(share, jnp.float32),
            pltpu.VMEM(share, jnp.float32),
            pltpu.VMEM(share, jnp.float32),
            dma(()),
            dma((groups,)),
            dma((n_rows,)),
            dma((n_rows,)),
        ],
        compiler_params=pltpu.CompilerParams(collective_id=1, has_side_effects=True),
    )(picks, rowv, colv)


def pick_table(row_cols, col_cols, targets):
    slots = row_cols.shape[1]
    count = col_cols.shape[0] * slots
    at = jnp.arange(count, dtype=jnp.int32)
    same = (targets[:, :, None, None] == (at // slots)[None, None, None, :]) & (
        row_cols[:, None, :, None] == col_cols.reshape(-1)[None, None, None, :]
    )
    found = count + jnp.sum(jnp.where(same, at - count, 0), axis=-1)
    return found.reshape(row_cols.shape[0], -1)


def per_device(p_vals, p_cols, c_cols):
    slots = p_cols.shape[1]
    half = c_cols.shape[2] // 2
    wanted = c_cols[:, 0, :] // ROWS
    targets = jnp.where(lax.axis_index("layer") == 0, wanted, jnp.roll(wanted, half, axis=1))
    padded = jnp.pad(p_cols[:, None, :], ((0, 0), (0, 0), (0, LANES - slots)))
    colv, colc, rowv, rowc = gather(p_vals, padded)
    picks = pick_table(rowc[:, 0, :slots], colc[:, 0, :slots], targets)
    return product(picks, rowv, colv, half)


def solution(mesh):
    return jax.shard_map(
        per_device,
        mesh=mesh,
        in_specs=(
            P(("prow", "pcol"), None, "layer"),
            P(("prow", "pcol"), "layer"),
            P("prow", "pcol", None),
        ),
        out_specs=P("prow", "pcol", None, "layer"),
        check_vma=False,
    )
```

time: 447 us -> 88 us (0.20)
  waiting for transfers between devices: 180 us -> 0 us
  blocking collectives: 123 us -> 0 us
  local copies, waits for them, and re-layouts: 86.6 us -> 5.37 us
  Pallas kernels: 0 us -> 79.2 us
  matrix products: 39.5 us -> 0 us
  between operations: 13.1 us -> 0.06 us
    all_gather x2 -> x0, waiting for transfers between devices: 135 us -> none  [the longest x1 135 us: per_device(): lax.all_gather(p_vals, 'prow', axis=0, tiled=True)]
    all_gather x2 -> x0, blocking collectives: 123 us -> none  [the longest x1 68.3 us: per_device(): lax.all_gather(p_cols, 'prow', axis=0, tiled=True)]
    pallas_call x0 -> x2, Pallas kernels: none -> 79.2 us  [the longest x1 58.2 us: gather(): pl.pallas_call(gather_kernel, name='gather_both', out_shape=(jax.ShapeDty...]
    gather x48 -> x0, local copies, waits for them, and re-layouts: 64.3 us -> none  [the longest x32 55.5 us: one_row(): picked = jnp.take(col_vals, wanted, axis=0)]
    unnamed x4 -> x0, waiting for transfers between devices: 45.6 us -> none
    dot_general x32 -> x0, matrix products: 39.5 us -> none  [the longest x16 29.5 us: one_row(): jnp.einsum('xk,oyk->xoy', row_block, chosen, preferred_element_type=jnp.f...]
    dot_general x16 -> x0, local copies, waits for them, and re-layouts: 14.6 us -> none  [one_row(): jnp.einsum('xk,oyk->xoy', row_block, chosen, preferred_element_type=jnp.f...]
    unnamed x4 -> x1, local copies, waits for them, and re-layouts: 7.37 us -> 1.88 us
  transfers between devices with their start and end apart: 3 -> 0, of which waited for: 2 -> 0; matrix products, arithmetic and copies ran while one was open for 0% -> 0% of each run, Pallas kernels for 0% -> 0%
where the time goes in v1:
time: 88 us; the launch traced here: 87.6 us
  Pallas kernels  79.2 us (90%)
  local copies, waits for them, and re-layouts  5.37 us (6%)
  other arithmetic  2.9 us (3%)
    pallas_call x1, Pallas kernels, gather(): pl.pallas_call(gather_kernel, name='gather_both', out_shape=(jax.ShapeDty...  58.2 us
    pallas_call x1, Pallas kernels, product(): pl.pallas_call(product_kernel, name='pick_multiply_swap', out_shape=jax.S...  21 us
    unnamed x1, local copies, waits for them, and re-layouts  1.88 us

profile of v1, /device:TPU:1, one launch (start us, length us, event | category | flops | bytes accessed | tf_op | source)
XLA Modules:
  0.0 87.6 jit_solution(15129220347904157846)
XLA Ops:
  0.0 1.2 %pad.4.cols = s32[1,1,128]{2,1,0:T(1,128)} pad(s32[1,1,12]{2,1,0:T(1,128)} %bitcast.24, s32[]{:T(128)} %constant.26.clone.1), padding=0_0x0_0x0_116 | pad | bytes 564 | tf_op jit(solution)/shard_map/jit(_pad)/pad | solution.py:307
  1.2 0.7 add_select_fusion
  1.9 0.7 add_select_fusion.1
  2.6 0.1 broadcast_compare_fusion.1
  2.7 58.2 %gather_both.1 = (bf16[32,64,768]{2,1,0:T(8,128)(2,1)}, s32[32,1,128]{2,1,0:T(1,128)}, bf16[16,64,768]{2,1,0:T(8,128)(2,1)}, s32[16,1,128]{2,1,0:T(1,128)}) custom-call(bf16[1,64,768]{2,1,0:T(8,128)(2,1)} %vals.1, s32[1,1,128]{2,1,0:T(1,128)} %pad.4.cols), custom_call_target="tpu_custom_call" | custom-call | tf_op jit(solution)/shard_map/gather_both/pallas_call | solution.py:153
  60.9 0.8 copy.6
  61.7 0.8 slice_reduce_fusion
  62.5 0.1 eq.49
  62.6 0.1 broadcast_compare_fusion
  62.7 1.3 %select_reduce_fusion = s32[16,6,12]{0,2,1:T(8,128)S(1)} fusion(s32[384]{0:T(512)S(1)} %iota_add_fusion, pred[16,12,384]{2,0,1:T(8,128)(4,1)S(1)} %broadcast_compare_fusion, pred[16,6,384]{2,0,1:T(8,128)(4,1)S(1)} %broadcast_compare_fusion.1), kind=kLoop, calls=%fused_computation | loop fusion | flops 1325952 | bytes 116736 | tf_op jit(solution)/shard_map/reduce_sum | solution.py:298
  64.0 0.7 copy.8.picks
  64.7 21.0 %pick_multiply_swap.1 = bf16[16,1,64,192]{3,2,1,0:T(8,128)(2,1)} custom-call(s32[16,72]{1,0:T(8,128)} %copy.8.picks, bf16[16,64,768]{2,1,0:T(8,128)(2,1)} %get-tuple-element.11.rowv, bf16[32,64,768]{2,1,0:T(8,128)(2,1)} %get-tuple-element.12.colv), custom_call_target="tpu_custom_call" | custom-call | tf_op jit(solution)/shard_map/pick_multiply_swap/pallas_call | solution.py:264
  85.7 1.9 %copy.28 = bf16[16,1,64,192]{3,2,1,0:T(8,128)(2,1)} copy(bf16[16,1,64,192]{3,2,1,0:T(8,128)(2,1)} %pick_multiply_swap.1) | data formatting | bytes 786432
  (5 shorter events, 0.0 us)

commit v2 on v1

--- a/solution.py
+++ b/solution.py
@@ -16,91 +16,133 @@
     me_q = lax.axis_index("pcol")
     x, z = me_p // NZ, me_p % NZ
     y, h = me_q // NH, me_q % NH
-
-    def on_p(dx, dz):
-        return (x + dx + NX) % NX * NZ + (z + dz + NZ) % NZ
-
-    def on_q(dy, dh):
-        return (y + dy + NY) % NY * NH + (h + dh) % NH
+    peer_z = (z, z + 1 - 2 * (z % 2), (z + 2) % NZ, NZ - 1 - z)
+
+    def on_p(dx, q):
+        return (x + dx + NX) % NX * NZ + peer_z[q]
+
+    def on_q(dy, p):
+        return (y + dy + NY) % NY * NH + (h + p) % NH
 
     barrier = pltpu.get_barrier_semaphore()
     partners = [{"prow": on_p(0, k)} for k in range(1, NZ)]
     partners += [{"prow": on_p(1, 0)}, {"prow": on_p(-1, 0)}]
-    partners += [{"pcol": on_q(0, 1)}, {"pcol": on_q(1, 0)}, {"pcol": on_q(-1, 0)}]
+    partners += [{"pcol": on_q(1, 0)}, {"pcol": on_q(-1, 0)}]
+    partners += [{"prow": on_p(0, k), "pcol": on_q(0, 1)} for k in range(NZ)]
     for who in partners:
         pl.semaphore_signal(barrier, inc=1, device_id=who, device_id_type=MESH)
     pl.semaphore_wait(barrier, len(partners))
 
-    def copies(dst_v, dst_c, slot, own, sends, recvs, sid, who):
-        src_v = vals.at[0] if own else dst_v.at[slot]
-        src_c = cols.at[0] if own else dst_c.at[slot]
+    def copies(pairs, sends, recvs, sid, who):
         return [
             pltpu.make_async_remote_copy(
                 src_ref=src,
-                dst_ref=dst.at[slot],
+                dst_ref=dst,
                 send_sem=sends.at[k, sid],
                 recv_sem=recvs.at[k, sid],
                 device_id=who,
                 device_id_type=MESH,
             )
-            for k, (src, dst) in enumerate(((src_c, dst_c), (src_v, dst_v)))
+            for k, (src, dst) in enumerate(pairs)
         ]
 
     sent = []
 
+    def copies_a(slot, own, sid, who):
+        src_c, src_v = (cols.at[0], vals.at[0]) if own else (colc.at[slot], colv.at[slot])
+        return copies(((src_c, colc.at[slot]), (src_v, colv.at[slot])), a_send, a_recv, sid, {"prow": who})
+
+    def copies_b(slot, own, sid, who):
+        src_c, src_v = (cols.at[0], vals.at[0]) if own else (rowc.at[slot], rowv.at[slot])
+        return copies(((src_c, rowc.at[slot]), (src_v, rowv.at[slot])), b_send, b_recv, sid, {"pcol": who})
+
     def send_a(slot, own, sid, who):
-        for c in copies(colv, colc, slot, own, a_send, a_recv, sid, {"prow": who}):
+        for c in copies_a(slot, own, sid, who):
             c.start()
             sent.append(c)
 
     def send_b(slot, own, sid, who):
-        for c in copies(rowv, rowc, slot, own, b_send, b_recv, sid, {"pcol": who}):
+        for c in copies_b(slot, own, sid, who):
             c.start()
             sent.append(c)
 
     def recv_a(slot, sid):
-        for c in copies(colv, colc, slot, False, a_send, a_recv, sid, {"prow": on_p(1, 0)}):
+        for c in copies_a(slot, False, sid, on_p(1, 0)):
             c.wait_recv()
 
     def recv_b(slot, sid):
-        for c in copies(rowv, rowc, slot, False, b_send, b_recv, sid, {"pcol": on_q(1, 0)}):
+        for c in copies_b(slot, False, sid, on_q(1, 0)):
             c.wait_recv()
 
-    def a_right(d, q):
-        return NZ + (d - 1) * NZ + q
-
-    def a_left(d, q):
-        return NZ + (NX // 2) * NZ + (d - 1) * NZ + q
-
-    def b_right(d, p):
-        return 1 + (d - 1) * NH + p
-
-    def b_left(d, p):
-        return 1 + (NY // 2) * NH + (d - 1) * NH + p
-
-    def forward_a(slot, own, d, q):
-        if d < NX // 2 - 1 or q < NZ // 2:
-            send_a(slot, own, a_right(d + 1, q), on_p(1, 0))
-
-    def forward_a_left(slot, own, d, q):
-        if d < NX // 2 - 1 or q >= NZ // 2:
-            send_a(slot, own, a_left(d + 1, q), on_p(-1, 0))
-
-    def forward_b(slot, own, d, p):
-        if d < NY // 2 - 1 or p == 0:
-            send_b(slot, own, b_right(d + 1, p), on_q(1, 0))
-
-    def forward_b_left(slot, own, d, p):
-        if d < NY // 2 - 1 or p == 1:
-            send_b(slot, own, b_left(d + 1, p), on_q(-1, 0))
-
-    forward_a(me_p, True, 0, 0)
-    forward_a_left(me_p, True, 0, 0)
-    forward_b(me_q, True, 0, 0)
-    forward_b_left(me_q, True, 0, 0)
-    for k in range(1, NZ):
-        send_a(me_p, True, k, on_p(0, k))
-    send_b(me_q, True, 0, on_q(0, 1))
+    half_x, half_y = NX // 2, NY // 2
+
+    def a_id(way, d, q):
+        return NZ + (way * half_x + d - 1) * NZ + q
+
+    def b_id(way, d, p):
+        return 1 + (way * half_y + d - 1) * NH + p
+
+    def goes_a(way, d, q):
+        return d < half_x or (q >= NZ // 2) == (way == 1)
+
+    def goes_b(way, d, p):
+        return d < half_y or p == way
+
+    def forward_a(way, d, q, own=False):
+        if goes_a(way, d + 1, q) and d < half_x:
+            step = -1 if way else 1
+            send_a(on_p(-step * d, q), own, a_id(way, d + 1, q), on_p(step, 0))
+
+    def forward_b(way, d, p, own=False):
+        if goes_b(way, d + 1, p) and d < half_y:
+            step = -1 if way else 1
+            send_b(on_q(-step * d, p), own, b_id(way, d + 1, p), on_q(step, 0))
+
+    def take_a(d, q):
+        if d == 0:
+            recv_a(on_p(0, q), q)
+        for way in (0, 1):
+            if d > 0 and goes_a(way, d, q):
+                recv_a(on_p(d if way else -d, q), a_id(way, d, q))
+                forward_a(way, d, q)
+            if d == 0:
+                forward_a(way, 0, q)
+
+    def take_b(d, p):
+        if d == 0:
+            recv_b(on_q(0, 1), 0)
+        for way in (0, 1):
+            if d > 0 and goes_b(way, d, p):
+                recv_b(on_q(d if way else -d, p), b_id(way, d, p))
+                forward_b(way, d, p)
+            if d == 0:
+                forward_b(way, 0, p)
+
+    edge = z % (NZ - 1) == 0
+
+    def cross(q):
+        @pl.when(edge)
+        def _():
+            for k, (src, dst) in enumerate(
+                ((colc.at[on_p(0, q)], rowc.at[me_q]), (colv.at[on_p(0, q)], rowv.at[me_q]))
+            ):
+                cross_copy(q, k, src, dst).start()
+
+    def cross_copy(q, k, src, dst):
+        return pltpu.make_async_remote_copy(
+            src_ref=src,
+            dst_ref=dst,
+            send_sem=own_sem.at[4 + 2 * (q - 2) + k],
+            recv_sem=b_recv.at[k, 0],
+            device_id={"prow": on_p(0, q), "pcol": on_q(0, 1)},
+            device_id_type=MESH,
+        )
+
+    for q in range(1, NZ):
+        send_a(me_p, True, q, on_p(0, q))
+    for way in (0, 1):
+        forward_a(way, 0, 0, True)
+        forward_b(way, 0, 0, True)
     own_copies = [
         pltpu.make_async_copy(vals.at[0], colv.at[me_p], own_sem.at[0]),
         pltpu.make_async_copy(cols.at[0], colc.at[me_p], own_sem.at[1]),
@@ -110,39 +152,48 @@
     for c in own_copies:
         c.start()
 
-    for q in range(1, NZ):
-        recv_a(on_p(0, -q), q)
-        forward_a(on_p(0, -q), False, 0, q)
-        forward_a_left(on_p(0, -q), False, 0, q)
-    recv_b(on_q(0, 1), 0)
-    forward_b(on_q(0, 1), False, 0, 1)
-    forward_b_left(on_q(0, 1), False, 0, 1)
-
-    for d in range(1, NX // 2 + 1):
-        last = d == NX // 2
-        for q in range(NZ):
-            if not last or q < NZ // 2:
-                recv_a(on_p(-d, -q), a_right(d, q))
-                if not last:
-                    forward_a(on_p(-d, -q), False, d, q)
-            if not last or q >= NZ // 2:
-                recv_a(on_p(d, -q), a_left(d, q))
-                if not last:
-                    forward_a_left(on_p(d, -q), False, d, q)
-            if q % 2 == 1:
-                p = q // 2
-                if not last or p == 0:
-                    recv_b(on_q(-d, p), b_right(d, p))
-                    if not last:
-                        forward_b(on_q(-d, p), False, d, p)
-                if not last or p == 1:
-                    recv_b(on_q(d, p), b_left(d, p))
-                    if not last:
-                        forward_b_left(on_q(d, p), False, d, p)
+    take_a(1, 0)
+    take_b(1, 0)
+    take_a(0, 1)
+    take_a(2, 0)
+    take_b(2, 0)
+    take_a(0, 2)
+    cross(2)
+    take_a(1, 1)
+    take_a(0, 3)
+    cross(3)
+    take_a(1, 2)
+    take_a(2, 1)
+    take_b(3, 0)
+    take_b(0, 1)
+    take_a(3, 0)
+    take_a(1, 3)
+    take_b(1, 1)
+    take_b(4, 0)
+    take_a(2, 2)
+    take_a(3, 1)
+    take_b(2, 1)
+    take_a(2, 3)
+    take_a(4, 0)
+    take_a(3, 2)
+    take_b(3, 1)
+    take_a(4, 1)
+    take_a(3, 3)
+    take_a(4, 2)
+    take_b(4, 1)
+    take_a(4, 3)
     for c in own_copies:
         c.wait()
     for c in sent:
         c.wait_send()
+
+    @pl.when(edge)
+    def _():
+        for q in (2, 3):
+            for k, (src, dst) in enumerate(
+                ((colc.at[on_p(0, q)], rowc.at[me_q]), (colv.at[on_p(0, q)], rowv.at[me_q]))
+            ):
+                cross_copy(q, k, src, dst).wait_send()
 
 
 def gather(vals, cols):
@@ -161,7 +212,7 @@
         ),
         in_specs=[pl.BlockSpec(memory_space=pltpu.VMEM)] * 2,
         out_specs=[pl.BlockSpec(memory_space=pl.ANY)] * 4,
-        scratch_shapes=[dma((2, n_a)), dma((2, n_a)), dma((2, n_b)), dma((2, n_b)), dma((4,))],
+        scratch_shapes=[dma((2, n_a)), dma((2, n_a)), dma((2, n_b)), dma((2, n_b)), dma((8,))],
         compiler_params=pltpu.CompilerParams(collective_id=0, has_side_effects=True),
     )(vals, cols)
 

time: 88 us -> 88.9 us (1.010)
  Pallas kernels: 79.2 us -> 80.1 us
    pallas_call x1, Pallas kernels: 21 us -> 24.7 us  [product(): pl.pallas_call(product_kernel, name='pick_multiply_swap', out_shape=jax.S...]
    pallas_call x1, Pallas kernels: 58.2 us -> 55.4 us  [gather(): pl.pallas_call(gather_kernel, name='gather_both', out_shape=(jax.ShapeDty...]
where the time goes in v2:
time: 88.9 us; the launch traced here: 88.5 us
  Pallas kernels  80.1 us (90%)
  local copies, waits for them, and re-layouts  5.37 us (6%)
  other arithmetic  2.9 us (3%)
    pallas_call x1, Pallas kernels, gather(): pl.pallas_call(gather_kernel, name='gather_both', out_shape=(jax.ShapeDty...  55.4 us
    pallas_call x1, Pallas kernels, product(): pl.pallas_call(product_kernel, name='pick_multiply_swap', out_shape=jax.S...  24.7 us
    unnamed x1, local copies, waits for them, and re-layouts  1.88 us

profile of v2, /device:TPU:1, one launch (start us, length us, event | category | flops | bytes accessed | tf_op | source)
XLA Modules:
  0.0 88.5 jit_solution(16805946377717636372)
XLA Ops:
  0.0 1.2 %pad.4.cols = s32[1,1,128]{2,1,0:T(1,128)} pad(s32[1,1,12]{2,1,0:T(1,128)} %bitcast.24, s32[]{:T(128)} %constant.26.clone.1), padding=0_0x0_0x0_116 | pad | bytes 564 | tf_op jit(solution)/shard_map/jit(_pad)/pad | solution.py:358
  1.2 0.7 add_select_fusion
  1.9 0.7 add_select_fusion.1
  2.6 0.1 broadcast_compare_fusion.1
  2.7 55.4 %gather_both.1 = (bf16[32,64,768]{2,1,0:T(8,128)(2,1)}, s32[32,1,128]{2,1,0:T(1,128)}, bf16[16,64,768]{2,1,0:T(8,128)(2,1)}, s32[16,1,128]{2,1,0:T(1,128)}) custom-call(bf16[1,64,768]{2,1,0:T(8,128)(2,1)} %vals.1, s32[1,1,128]{2,1,0:T(1,128)} %pad.4.cols), custom_call_target="tpu_custom_call" | custom-call | tf_op jit(solution)/shard_map/gather_both/pallas_call | solution.py:204
  58.1 0.8 copy.6
  58.9 0.8 slice_reduce_fusion
  59.7 0.1 eq.49
  59.8 0.1 broadcast_compare_fusion
  59.9 1.3 %select_reduce_fusion = s32[16,6,12]{0,2,1:T(8,128)S(1)} fusion(s32[384]{0:T(512)S(1)} %iota_add_fusion, pred[16,12,384]{2,0,1:T(8,128)(4,1)S(1)} %broadcast_compare_fusion, pred[16,6,384]{2,0,1:T(8,128)(4,1)S(1)} %broadcast_compare_fusion.1), kind=kLoop, calls=%fused_computation | loop fusion | flops 1325952 | bytes 116736 | tf_op jit(solution)/shard_map/reduce_sum | solution.py:349
  61.2 0.7 copy.8.picks
  61.9 24.7 %pick_multiply_swap.1 = bf16[16,1,64,192]{3,2,1,0:T(8,128)(2,1)} custom-call(s32[16,72]{1,0:T(8,128)} %copy.8.picks, bf16[16,64,768]{2,1,0:T(8,128)(2,1)} %get-tuple-element.11.rowv, bf16[32,64,768]{2,1,0:T(8,128)(2,1)} %get-tuple-element.12.colv), custom_call_target="tpu_custom_call" | custom-call | tf_op jit(solution)/shard_map/pick_multiply_swap/pallas_call | solution.py:315
  86.6 1.9 %copy.28 = bf16[16,1,64,192]{3,2,1,0:T(8,128)(2,1)} copy(bf16[16,1,64,192]{3,2,1,0:T(8,128)(2,1)} %pick_multiply_swap.1) | data formatting | bytes 786432
  (5 shorter events, 0.0 us)

commit v3 on v2

--- a/solution.py
+++ b/solution.py
@@ -9,9 +9,10 @@
 NX, NZ, NY, NH = 8, 4, 8, 2
 COLS, ROWS = NX * NZ, NY * NH
 LANES = 128
-
-
-def gather_kernel(vals, cols, colv, colc, rowv, rowc, a_send, a_recv, b_send, b_recv, own_sem):
+TAIL = 16
+
+
+def gather_kernel(vals, cols, colv, colc, rowv, rowc, a_send, a_recv, b_send, b_recv, own_sem, t_send, t_recv):
     me_p = lax.axis_index("prow")
     me_q = lax.axis_index("pcol")
     x, z = me_p // NZ, me_p % NZ
@@ -48,16 +49,39 @@
 
     sent = []
 
-    def copies_a(slot, own, sid, who):
+    head = pl.ds(0, vals.shape[1] - TAIL)
+    tail = pl.ds(vals.shape[1] - TAIL, TAIL)
+
+    def copies_a(slot, own, sid, who, part):
         src_c, src_v = (cols.at[0], vals.at[0]) if own else (colc.at[slot], colv.at[slot])
-        return copies(((src_c, colc.at[slot]), (src_v, colv.at[slot])), a_send, a_recv, sid, {"prow": who})
+        dst_v = colv.at[slot]
+        if part:
+            src_v, dst_v = src_v.at[head], dst_v.at[head]
+        return copies(((src_c, colc.at[slot]), (src_v, dst_v)), a_send, a_recv, sid, {"prow": who})
+
+    def tail_copy(dx, q, slot):
+        k = (dx - 1) * (NZ - 1) + q - 1
+        return pltpu.make_async_remote_copy(
+            src_ref=colv.at[slot, tail],
+            dst_ref=colv.at[slot, tail],
+            send_sem=t_send.at[k],
+            recv_sem=t_recv.at[k],
+            device_id={"prow": on_p(0, q)},
+            device_id_type=MESH,
+        )
+
+    def spread_tail(dx):
+        for q in range(1, NZ):
+            c = tail_copy(dx, q, on_p(dx, 0))
+            c.start()
+            sent.append(c)
 
     def copies_b(slot, own, sid, who):
         src_c, src_v = (cols.at[0], vals.at[0]) if own else (rowc.at[slot], rowv.at[slot])
         return copies(((src_c, rowc.at[slot]), (src_v, rowv.at[slot])), b_send, b_recv, sid, {"pcol": who})
 
-    def send_a(slot, own, sid, who):
-        for c in copies_a(slot, own, sid, who):
+    def send_a(slot, own, sid, who, part=False):
+        for c in copies_a(slot, own, sid, who, part):
             c.start()
             sent.append(c)
 
@@ -66,8 +90,8 @@
             c.start()
             sent.append(c)
 
-    def recv_a(slot, sid):
-        for c in copies_a(slot, False, sid, on_p(1, 0)):
+    def recv_a(slot, sid, part=False):
+        for c in copies_a(slot, False, sid, on_p(1, 0), part):
             c.wait_recv()
 
     def recv_b(slot, sid):
@@ -91,7 +115,7 @@
     def forward_a(way, d, q, own=False):
         if goes_a(way, d + 1, q) and d < half_x:
             step = -1 if way else 1
-            send_a(on_p(-step * d, q), own, a_id(way, d + 1, q), on_p(step, 0))
+            send_a(on_p(-step * d, q), own, a_id(way, d + 1, q), on_p(step, 0), q > 0)
 
     def forward_b(way, d, p, own=False):
         if goes_b(way, d + 1, p) and d < half_y:
@@ -103,8 +127,10 @@
             recv_a(on_p(0, q), q)
         for way in (0, 1):
             if d > 0 and goes_a(way, d, q):
-                recv_a(on_p(d if way else -d, q), a_id(way, d, q))
+                recv_a(on_p(d if way else -d, q), a_id(way, d, q), q > 0)
                 forward_a(way, d, q)
+                if q == 0:
+                    spread_tail(d if way else NX - d)
             if d == 0:
                 forward_a(way, 0, q)
 
@@ -182,6 +208,9 @@
     take_a(4, 2)
     take_b(4, 1)
     take_a(4, 3)
+    for dx in range(1, NX):
+        for q in range(1, NZ):
+            tail_copy(dx, q, on_p(dx, q)).wait_recv()
     for c in own_copies:
         c.wait()
     for c in sent:
@@ -199,6 +228,7 @@
 def gather(vals, cols):
     n_a = NZ + NX * NZ
     n_b = 1 + NY * NH
+    n_t = (NX - 1) * (NZ - 1)
     dma = pltpu.SemaphoreType.DMA
     shape = vals.shape[1:]
     return pl.pallas_call(
@@ -212,7 +242,7 @@
         ),
         in_specs=[pl.BlockSpec(memory_space=pltpu.VMEM)] * 2,
         out_specs=[pl.BlockSpec(memory_space=pl.ANY)] * 4,
-        scratch_shapes=[dma((2, n_a)), dma((2, n_a)), dma((2, n_b)), dma((2, n_b)), dma((8,))],
+        scratch_shapes=[dma((2, n_a)), dma((2, n_a)), dma((2, n_b)), dma((2, n_b)), dma((8,)), dma((n_t,)), dma((n_t,))],
         compiler_params=pltpu.CompilerParams(collective_id=0, has_side_effects=True),
     )(vals, cols)
 

time: 88.9 us -> 87.3 us (0.982)
  Pallas kernels: 80.1 us -> 78.5 us
    pallas_call x1, Pallas kernels: 55.4 us -> 53.6 us  [gather(): pl.pallas_call(gather_kernel, name='gather_both', out_shape=(jax.ShapeDty...]
where the time goes in v3:
time: 87.3 us; the launch traced here: 86.8 us
  Pallas kernels  78.5 us (90%)
  local copies, waits for them, and re-layouts  5.37 us (6%)
  other arithmetic  2.9 us (3%)
    pallas_call x1, Pallas kernels, gather(): pl.pallas_call(gather_kernel, name='gather_both', out_shape=(jax.ShapeDty...  53.6 us
    pallas_call x1, Pallas kernels, product(): pl.pallas_call(product_kernel, name='pick_multiply_swap', out_shape=jax.S...  24.8 us
    unnamed x1, local copies, waits for them, and re-layouts  1.88 us

profile of v3, /device:TPU:1, one launch (start us, length us, event | category | flops | bytes accessed | tf_op | source)
XLA Modules:
  0.0 86.8 jit_solution(11281572532275250198)
XLA Ops:
  0.0 1.2 %pad.4.cols = s32[1,1,128]{2,1,0:T(1,128)} pad(s32[1,1,12]{2,1,0:T(1,128)} %bitcast.24, s32[]{:T(128)} %constant.26.clone.1), padding=0_0x0_0x0_116 | pad | bytes 564 | tf_op jit(solution)/shard_map/jit(_pad)/pad | solution.py:388
  1.2 0.7 add_select_fusion
  1.9 0.7 add_select_fusion.1
  2.6 0.1 broadcast_compare_fusion.1
  2.7 53.6 %gather_both.1 = (bf16[32,64,768]{2,1,0:T(8,128)(2,1)}, s32[32,1,128]{2,1,0:T(1,128)}, bf16[16,64,768]{2,1,0:T(8,128)(2,1)}, s32[16,1,128]{2,1,0:T(1,128)}) custom-call(bf16[1,64,768]{2,1,0:T(8,128)(2,1)} %vals.1, s32[1,1,128]{2,1,0:T(1,128)} %pad.4.cols), custom_call_target="tpu_custom_call" | custom-call | tf_op jit(solution)/shard_map/gather_both/pallas_call | solution.py:234
  56.3 0.8 copy.6
  57.1 0.8 slice_reduce_fusion
  57.9 0.1 eq.49
  58.0 0.1 broadcast_compare_fusion
  58.1 1.3 %select_reduce_fusion = s32[16,6,12]{0,2,1:T(8,128)S(1)} fusion(s32[384]{0:T(512)S(1)} %iota_add_fusion, pred[16,12,384]{2,0,1:T(8,128)(4,1)S(1)} %broadcast_compare_fusion, pred[16,6,384]{2,0,1:T(8,128)(4,1)S(1)} %broadcast_compare_fusion.1), kind=kLoop, calls=%fused_computation | loop fusion | flops 1325952 | bytes 116736 | tf_op jit(solution)/shard_map/reduce_sum | solution.py:379
  59.4 0.7 copy.8.picks
  60.1 24.8 %pick_multiply_swap.1 = bf16[16,1,64,192]{3,2,1,0:T(8,128)(2,1)} custom-call(s32[16,72]{1,0:T(8,128)} %copy.8.picks, bf16[16,64,768]{2,1,0:T(8,128)(2,1)} %get-tuple-element.11.rowv, bf16[32,64,768]{2,1,0:T(8,128)(2,1)} %get-tuple-element.12.colv), custom_call_target="tpu_custom_call" | custom-call | tf_op jit(solution)/shard_map/pick_multiply_swap/pallas_call | solution.py:345
  84.9 1.9 %copy.28 = bf16[16,1,64,192]{3,2,1,0:T(8,128)(2,1)} copy(bf16[16,1,64,192]{3,2,1,0:T(8,128)(2,1)} %pick_multiply_swap.1) | data formatting | bytes 786432
  (5 shorter events, 0.0 us)

commit v4 on v3

v4 whole, which is shorter than its diff:
```python
import jax
import jax.numpy as jnp
from jax import lax
from jax.experimental import pallas as pl
from jax.experimental.pallas import tpu as pltpu
from jax.sharding import PartitionSpec as P

MESH = pl.DeviceIdType.MESH
NX, NZ, NY, NH = 8, 4, 8, 2
COLS, ROWS = NX * NZ, NY * NH
LANES = 128
TAIL = 16


def fused_kernel(
    vals, cols, wanted, out, colv, colc, rowv, rowc, twice, near, far, found, picks, chosen, own, send, recv,
    a_send, a_recv, b_send, b_recv, own_sem, t_send, t_recv, s_send, s_recv,
):
    me_p = lax.axis_index("prow")
    me_q = lax.axis_index("pcol")
    me_l = lax.axis_index("layer")
    x, z = me_p // NZ, me_p % NZ
    y, h = me_q // NH, me_q % NH
    peer_z = (z, z + 1 - 2 * (z % 2), (z + 2) % NZ, NZ - 1 - z)
    edge_len, width = vals.shape[1:]
    slots = cols.shape[2]
    kept = wanted.shape[1]
    half = kept // 2
    low = lax.broadcasted_iota(jnp.int32, (edge_len, LANES), 1) < edge_len

    def on_p(dx, q):
        return (x + dx + NX) % NX * NZ + peer_z[q]

    def on_q(dy, p):
        return (y + dy + NY) % NY * NH + (h + p) % NH

    barrier = pltpu.get_barrier_semaphore()
    partners = [{"prow": on_p(0, k)} for k in range(1, NZ)]
    partners += [{"prow": on_p(1, 0)}, {"prow": on_p(-1, 0)}]
    partners += [{"pcol": on_q(1, 0)}, {"pcol": on_q(-1, 0)}]
    partners += [{"prow": on_p(0, k), "pcol": on_q(0, 1)} for k in range(NZ)]
    other = {"layer": 1 - me_l}
    partners += [other]
    for who in partners:
        pl.semaphore_signal(barrier, inc=1, device_id=who, device_id_type=MESH)
    pl.semaphore_wait(barrier, len(partners))

    def copies(pairs, sends, recvs, sid, who):
        return [
            pltpu.make_async_remote_copy(
                src_ref=src,
                dst_ref=dst,
                send_sem=sends.at[k, sid],
                recv_sem=recvs.at[k, sid],
                device_id=who,
                device_id_type=MESH,
            )
            for k, (src, dst) in enumerate(pairs)
        ]

    sent = []

    head = pl.ds(0, vals.shape[1] - TAIL)
    tail = pl.ds(vals.shape[1] - TAIL, TAIL)

    def copies_a(slot, own, sid, who, part):
        src_c, src_v = (cols.at[0], vals.at[0]) if own else (colc.at[slot], colv.at[slot])
        dst_v = colv.at[slot]
        if part:
            src_v, dst_v = src_v.at[head], dst_v.at[head]
            return copies(((src_v, dst_v),), a_send, a_recv, sid, {"prow": who})
        return copies(((src_v, dst_v), (src_c, colc.at[slot])), a_send, a_recv, sid, {"prow": who})

    def copies_b(slot, own, sid, who):
        src_c, src_v = (cols.at[0], vals.at[0]) if own else (rowc.at[slot], rowv.at[slot])
        return copies(((src_v, rowv.at[slot]), (src_c, rowc.at[slot])), b_send, b_recv, sid, {"pcol": who})

    def tail_copies(dx, q, slot):
        k = (dx - 1) * (NZ - 1) + q - 1
        pairs = ((colv.at[slot, tail], colv.at[slot, tail]), (colc.at[slot], colc.at[slot]))
        return copies(pairs, t_send, t_recv, k, {"prow": on_p(0, q)})

    def spread_tail(dx):
        for q in range(1, NZ):
            for c in tail_copies(dx, q, on_p(dx, 0)):
                c.start()
                sent.append(c)

    def spread(src, slot, first, count):
        mask = low[:count]

        def pair_of(b, carry):
            block = src[pl.ds(first, count), pl.ds(pl.multiple_of(b * LANES, LANES), LANES)]
            turned = jnp.concatenate([block[:, edge_len:], block[:, :edge_len]], axis=1)
            twice[slot, 2 * b, pl.ds(first, count), :] = jnp.where(mask, block, turned)
            twice[slot, 2 * b + 1, pl.ds(first, count), :] = jnp.where(mask, turned, block)
            return carry

        lax.fori_loop(0, slots // 2, pair_of, 0)

    def send_a(slot, own, sid, who, part=False):
        for c in copies_a(slot, own, sid, who, part):
            c.start()
            sent.append(c)

    def send_b(slot, own, sid, who):
        for c in copies_b(slot, own, sid, who):
            c.start()
            sent.append(c)

    def recv_a(slot, sid, part=False):
        for c in copies_a(slot, False, sid, on_p(1, 0), part):
            c.wait_recv()

    def recv_b(slot, sid):
        for c in copies_b(slot, False, sid, on_q(1, 0)):
            c.wait_recv()

    half_x, half_y = NX // 2, NY // 2

    def a_id(way, d, q):
        return NZ + (way * half_x + d - 1) * NZ + q

    def b_id(way, d, p):
        return 1 + (way * half_y + d - 1) * NH + p

    def goes_a(way, d, q):
        return d < half_x or (q >= NZ // 2) == (way == 1)

    def goes_b(way, d, p):
        return d < half_y or p == way

    def forward_a(way, d, q, own=False):
        if goes_a(way, d + 1, q) and d < half_x:
            step = -1 if way else 1
            send_a(on_p(-step * d, q), own, a_id(way, d + 1, q), on_p(step, 0), q > 0)

    def forward_b(way, d, p, own=False):
        if goes_b(way, d + 1, p) and d < half_y:
            step = -1 if way else 1
            send_b(on_q(-step * d, p), own, b_id(way, d + 1, p), on_q(step, 0))

    def take_a(d, q):
        if d == 0:
            recv_a(on_p(0, q), q)
        for way in (0, 1):
            if d > 0 and goes_a(way, d, q):
                recv_a(on_p(d if way else -d, q), a_id(way, d, q), q > 0)
                forward_a(way, d, q)
                if q == 0:
                    spread_tail(d if way else NX - d)
            if d == 0:
                forward_a(way, 0, q)
        for way in (0, 1):
            if (d > 0 and goes_a(way, d, q)) or (d == 0 and way == 0):
                slot = on_p(d if way else -d, q)
                spread(colv.at[slot], slot, 0, edge_len - TAIL if q and d else edge_len)

    def take_b(d, p):
        if d == 0:
            recv_b(on_q(0, 1), 0)
        for way in (0, 1):
            if d > 0 and goes_b(way, d, p):
                recv_b(on_q(d if way else -d, p), b_id(way, d, p))
                forward_b(way, d, p)
            if d == 0:
                forward_b(way, 0, p)

    edge = z % (NZ - 1) == 0

    def cross(q):
        @pl.when(edge)
        def _():
            for k, (src, dst) in enumerate(
                ((colv.at[on_p(0, q)], rowv.at[me_q]), (colc.at[on_p(0, q)], rowc.at[me_q]))
            ):
                cross_copy(q, k, src, dst).start()

    def cross_copy(q, k, src, dst):
        return pltpu.make_async_remote_copy(
            src_ref=src,
            dst_ref=dst,
            send_sem=own_sem.at[4 + 2 * (q - 2) + k],
            recv_sem=b_recv.at[k, 0],
            device_id={"prow": on_p(0, q), "pcol": on_q(0, 1)},
            device_id_type=MESH,
        )

    for q in range(1, NZ):
        send_a(me_p, True, q, on_p(0, q))
    for way in (0, 1):
        forward_a(way, 0, 0, True)
        forward_b(way, 0, 0, True)
    own_copies = [
        pltpu.make_async_copy(cols.at[0], colc.at[me_p], own_sem.at[1]),
        pltpu.make_async_copy(vals.at[0], rowv.at[me_q], own_sem.at[2]),
        pltpu.make_async_copy(cols.at[0], rowc.at[me_q], own_sem.at[3]),
    ]
    for c in own_copies:
        c.start()
    for j in range(COLS):
        twice[j, slots] = jnp.zeros((edge_len, LANES), twice.dtype)
    near[...] = jnp.zeros_like(near)
    far[...] = jnp.zeros_like(far)
    spread(vals.at[0], me_p, 0, edge_len)

    take_a(1, 0)
    take_b(1, 0)
    take_a(0, 1)
    take_a(2, 0)
    take_b(2, 0)
    take_a(0, 2)
    cross(2)
    take_a(1, 1)
    take_a(0, 3)
    cross(3)
    take_a(1, 2)
    take_a(2, 1)
    take_b(3, 0)
    take_b(0, 1)
    take_a(3, 0)
    take_a(1, 3)
    take_b(1, 1)
    take_b(4, 0)
    take_a(2, 2)
    take_a(3, 1)
    take_b(2, 1)
    take_a(2, 3)
    take_a(4, 0)
    take_a(3, 2)
    take_b(3, 1)
    take_a(3, 3)
    take_a(4, 1)
    for c in own_copies:
        c.wait()
    take_b(4, 1)
    for dx in range(1, NX):
        for q in range(1, NZ):
            slot = on_p(dx, q)
            for c in tail_copies(dx, q, slot):
                c.wait_recv()
            spread(colv.at[slot], slot, edge_len - TAIL, TAIL)

    def target(i, side, o):
        return lax.div(wanted[i, (me_l + side) % 2 * half + o], ROWS)

    def line_up(i, carry):
        for side in (0, 1):
            for o in range(half):
                r = i * kept + side * half + o
                far[pl.ds(r, 1), pl.ds(0, slots)] = colc[target(i, side, o)]
                near[pl.ds(r, 1), pl.ds(0, slots)] = rowc[i]
        return carry

    n_rows = rowv.shape[0]
    lax.fori_loop(0, n_rows, line_up, 0)
    here, there = near[...], far[...]
    which = jnp.full(here.shape, slots, jnp.int32)
    for b in range(slots):
        which = jnp.where(there[:, b : b + 1] == here, b, which)
    found[...] = which
    to_scalars = pltpu.make_async_copy(found, picks, own_sem.at[0])
    to_scalars.start()
    take_a(4, 2)
    take_a(4, 3)
    to_scalars.wait()

    def swap(i):
        return pltpu.make_async_remote_copy(
            src_ref=send.at[i],
            dst_ref=recv.at[i],
            send_sem=s_send.at[i],
            recv_sem=s_recv.at[i],
            device_id=other,
            device_id_type=MESH,
        )

    def one_row(i, carry):
        a = rowv[i]
        for side, into in ((1, send), (0, own)):
            for o in range(half):
                r = i * kept + side * half + o
                t = target(i, side, o)
                for p in range(slots // 2):
                    first = twice[t, picks[r, 2 * p]]
                    second = twice[t, picks[r, 2 * p + 1]]
                    chosen[side, o * edge_len : (o + 1) * edge_len, p * LANES : (p + 1) * LANES] = jnp.where(
                        low, first, second
                    )
            into[i] = lax.dot_general(
                a, chosen[side], (((1,), (1,)), ((), ())), preferred_element_type=jnp.float32
            )
            if side == 1:

                @pl.when(i > 0)
                def _():
                    swap(i - 1).start()

        return carry

    lax.fori_loop(0, n_rows, one_row, 0)
    swap(n_rows - 1).start()

    def finish(i, carry):
        swap(i).wait_recv()
        out[i, 0] = (own[i] + recv[i]).astype(out.dtype)
        return carry

    lax.fori_loop(0, n_rows, finish, 0)

    def drain(i, carry):
        swap(i).wait_send()
        return carry

    lax.fori_loop(0, n_rows, drain, 0)
    for c in sent:
        c.wait_send()

    @pl.when(edge)
    def _():
        for q in (2, 3):
            for k, (src, dst) in enumerate(
                ((colv.at[on_p(0, q)], rowv.at[me_q]), (colc.at[on_p(0, q)], rowc.at[me_q]))
            ):
                cross_copy(q, k, src, dst).wait_send()


def fused(vals, cols, wanted):
    n_a = NZ + NX * NZ
    n_b = 1 + NY * NH
    n_t = (NX - 1) * (NZ - 1)
    dma = pltpu.SemaphoreType.DMA
    edge_len, width = vals.shape[1:]
    slots = cols.shape[2]
    n_rows, kept = wanted.shape
    half = kept // 2
    share = (n_rows, edge_len, half * edge_len)
    return pl.pallas_call(
        fused_kernel,
        name="gather_pick_multiply_swap",
        out_shape=jax.ShapeDtypeStruct((n_rows, 1, edge_len, half * edge_len), vals.dtype),
        in_specs=[
            pl.BlockSpec(memory_space=pltpu.VMEM),
            pl.BlockSpec(memory_space=pltpu.VMEM),
            pl.BlockSpec(memory_space=pltpu.SMEM),
        ],
        out_specs=pl.BlockSpec(memory_space=pltpu.VMEM),
        scratch_shapes=[
            pltpu.VMEM((COLS, edge_len, width), vals.dtype),
            pltpu.VMEM((COLS, 1, slots), jnp.int32),
            pltpu.VMEM((ROWS, edge_len, width), vals.dtype),
            pltpu.VMEM((ROWS, 1, slots), jnp.int32),
            pltpu.VMEM((COLS, slots + 1, edge_len, LANES), vals.dtype),
            pltpu.VMEM((n_rows * kept, LANES), jnp.int32),
            pltpu.VMEM((n_rows * kept, LANES), jnp.int32),
            pltpu.VMEM((n_rows * kept, LANES), jnp.int32),
            pltpu.SMEM((n_rows * kept, LANES), jnp.int32),
            pltpu.VMEM((2, half * edge_len, width), vals.dtype),
            pltpu.VMEM(share, jnp.float32),
            pltpu.VMEM(share, jnp.float32),
            pltpu.VMEM(share, jnp.float32),
            dma((2, n_a)),
            dma((2, n_a)),
            dma((2, n_b)),
            dma((2, n_b)),
            dma((8,)),
            dma((2, n_t)),
            dma((2, n_t)),
            dma((n_rows,)),
            dma((n_rows,)),
        ],
        compiler_params=pltpu.CompilerParams(collective_id=0, has_side_effects=True),
    )(vals, cols, wanted)


def per_device(p_vals, p_cols, c_cols):
    return fused(p_vals, p_cols[:, None, :], c_cols[:, 0, :])


def solution(mesh):
    return jax.shard_map(
        per_device,
        mesh=mesh,
        in_specs=(
            P(("prow", "pcol"), None, "layer"),
            P(("prow", "pcol"), "layer"),
            P("prow", "pcol", None),
        ),
        out_specs=P("prow", "pcol", None, "layer"),
        check_vma=False,
    )
```

time: 87.3 us -> 87.7 us (level)
  Pallas kernels: 78.5 us -> 83.9 us
  other arithmetic: 2.9 us -> 0 us
  local copies, waits for them, and re-layouts: 5.37 us -> 3.24 us
    pallas_call x2 -> x1, Pallas kernels: 78.5 us -> 83.9 us  [fused(): pl.pallas_call(fused_kernel, name='gather_pick_multiply_swap', out_shape=...]
    select_n x3 -> x0, other arithmetic: 1.4 us -> none  [the longest x1 0.69 us: per_device(): jnp.where(lax.axis_index('layer') == 0, wanted, jnp.roll(wanted, half, ax...]
    squeeze x0 -> x1, local copies, waits for them, and re-layouts: none -> 1.36 us  [per_device(): return fused(p_vals, p_cols[:, None, :], c_cols[:, 0, :])]
    reduce_sum x1 -> x0, other arithmetic: 1.3 us -> none  [pick_table(): found = count + jnp.sum(jnp.where(same, at - count, 0), axis=-1)]
    pad x1 -> x0, local copies, waits for them, and re-layouts: 1.17 us -> none  [per_device(): padded = jnp.pad(p_cols[:, None, :], ((0, 0), (0, 0), (0, LANES - slots)))]
    eq x2 -> x0, local copies, waits for them, and re-layouts: 0.88 us -> none  [pick_table(): row_cols[:, None, :, None] == col_cols.reshape(-1)[None, None, None, :]]
where the time goes in v4:
time: 87.7 us; the launch traced here: 87.2 us
  Pallas kernels  83.9 us (96%)
  local copies, waits for them, and re-layouts  3.24 us (4%)
    pallas_call x1, Pallas kernels, fused(): pl.pallas_call(fused_kernel, name='gather_pick_multiply_swap', out_shape=...  83.9 us
    unnamed x1, local copies, waits for them, and re-layouts  1.88 us

profile of v4, /device:TPU:1, one launch (start us, length us, event | category | flops | bytes accessed | tf_op | source)
XLA Modules:
  0.0 87.2 jit_solution(18394303554869676974)
XLA Ops:
  0.0 1.4 %copy.5 = s32[16,1,6]{2,0,1:T(8,128)} copy(s32[16,1,6]{0,1,2:T(1,128)} %param.5) | data formatting | bytes 768 | tf_op jit(solution)/shard_map/squeeze | solution.py:377
  1.4 83.9 %gather_pick_multiply_swap.1 = bf16[16,1,64,192]{3,2,1,0:T(8,128)(2,1)} custom-call(bf16[1,64,768]{2,1,0:T(8,128)(2,1)} %vals.1, s32[1,1,12]{2,1,0:T(1,128)} %bitcast.3, s32[16,6]{1,0:T(8,128)} %bitcast.2), custom_call_target="tpu_custom_call" | custom-call | tf_op jit(solution)/shard_map/gather_pick_multiply_swap/pallas_call | solution.py:338
  85.3 1.9 %copy.7 = bf16[16,1,64,192]{3,2,1,0:T(8,128)(2,1)} copy(bf16[16,1,64,192]{3,2,1,0:T(8,128)(2,1)} %gather_pick_multiply_swap.1) | data formatting | bytes 786432

commit v5 on v4

--- a/solution.py
+++ b/solution.py
@@ -24,7 +24,7 @@
     peer_z = (z, z + 1 - 2 * (z % 2), (z + 2) % NZ, NZ - 1 - z)
     edge_len, width = vals.shape[1:]
     slots = cols.shape[2]
-    kept = wanted.shape[1]
+    kept = wanted.shape[0]
     half = kept // 2
     low = lax.broadcasted_iota(jnp.int32, (edge_len, LANES), 1) < edge_len
 
@@ -86,17 +86,13 @@
                 c.start()
                 sent.append(c)
 
-    def spread(src, slot, first, count):
-        mask = low[:count]
-
-        def pair_of(b, carry):
-            block = src[pl.ds(first, count), pl.ds(pl.multiple_of(b * LANES, LANES), LANES)]
+    def spread(j, carry):
+        for b in range(slots // 2):
+            block = colv[j, :, b * LANES : (b + 1) * LANES]
             turned = jnp.concatenate([block[:, edge_len:], block[:, :edge_len]], axis=1)
-            twice[slot, 2 * b, pl.ds(first, count), :] = jnp.where(mask, block, turned)
-            twice[slot, 2 * b + 1, pl.ds(first, count), :] = jnp.where(mask, turned, block)
-            return carry
-
-        lax.fori_loop(0, slots // 2, pair_of, 0)
+            twice[j, 2 * b] = jnp.where(low, block, turned)
+            twice[j, 2 * b + 1] = jnp.where(low, turned, block)
+        return carry
 
     def send_a(slot, own, sid, who, part=False):
         for c in copies_a(slot, own, sid, who, part):
@@ -151,10 +147,6 @@
                     spread_tail(d if way else NX - d)
             if d == 0:
                 forward_a(way, 0, q)
-        for way in (0, 1):
-            if (d > 0 and goes_a(way, d, q)) or (d == 0 and way == 0):
-                slot = on_p(d if way else -d, q)
-                spread(colv.at[slot], slot, 0, edge_len - TAIL if q and d else edge_len)
 
     def take_b(d, p):
         if d == 0:
@@ -192,6 +184,7 @@
         forward_a(way, 0, 0, True)
         forward_b(way, 0, 0, True)
     own_copies = [
+        pltpu.make_async_copy(vals.at[0], colv.at[me_p], own_sem.at[0]),
         pltpu.make_async_copy(cols.at[0], colc.at[me_p], own_sem.at[1]),
         pltpu.make_async_copy(vals.at[0], rowv.at[me_q], own_sem.at[2]),
         pltpu.make_async_copy(cols.at[0], rowc.at[me_q], own_sem.at[3]),
@@ -202,7 +195,6 @@
         twice[j, slots] = jnp.zeros((edge_len, LANES), twice.dtype)
     near[...] = jnp.zeros_like(near)
     far[...] = jnp.zeros_like(far)
-    spread(vals.at[0], me_p, 0, edge_len)
 
     take_a(1, 0)
     take_b(1, 0)
@@ -239,10 +231,9 @@
             slot = on_p(dx, q)
             for c in tail_copies(dx, q, slot):
                 c.wait_recv()
-            spread(colv.at[slot], slot, edge_len - TAIL, TAIL)
 
     def target(i, side, o):
-        return lax.div(wanted[i, (me_l + side) % 2 * half + o], ROWS)
+        return lax.div(wanted[(me_l + side) % 2 * half + o, 0, i], ROWS)
 
     def line_up(i, carry):
         for side in (0, 1):
@@ -263,6 +254,7 @@
     to_scalars.start()
     take_a(4, 2)
     take_a(4, 3)
+    lax.fori_loop(0, COLS, spread, 0)
     to_scalars.wait()
 
     def swap(i):
@@ -275,31 +267,36 @@
             device_id_type=MESH,
         )
 
-    def one_row(i, carry):
-        a = rowv[i]
-        for side, into in ((1, send), (0, own)):
-            for o in range(half):
-                r = i * kept + side * half + o
-                t = target(i, side, o)
-                for p in range(slots // 2):
-                    first = twice[t, picks[r, 2 * p]]
-                    second = twice[t, picks[r, 2 * p + 1]]
-                    chosen[side, o * edge_len : (o + 1) * edge_len, p * LANES : (p + 1) * LANES] = jnp.where(
-                        low, first, second
-                    )
-            into[i] = lax.dot_general(
-                a, chosen[side], (((1,), (1,)), ((), ())), preferred_element_type=jnp.float32
-            )
-            if side == 1:
-
-                @pl.when(i > 0)
-                def _():
-                    swap(i - 1).start()
-
-        return carry
-
-    lax.fori_loop(0, n_rows, one_row, 0)
+    def one_row(side, into, i):
+        for o in range(half):
+            r = i * kept + side * half + o
+            t = target(i, side, o)
+            for p in range(slots // 2):
+                first = twice[t, picks[r, 2 * p]]
+                second = twice[t, picks[r, 2 * p + 1]]
+                chosen[side, o * edge_len : (o + 1) * edge_len, p * LANES : (p + 1) * LANES] = jnp.where(
+                    low, first, second
+                )
+        into[i] = lax.dot_general(
+            rowv[i], chosen[side], (((1,), (1,)), ((), ())), preferred_element_type=jnp.float32
+        )
+
+    def send_row(i, carry):
+        one_row(1, send, i)
+
+        @pl.when(i > 0)
+        def _():
+            swap(i - 1).start()
+
+        return carry
+
+    def own_row(i, carry):
+        one_row(0, own, i)
+        return carry
+
+    lax.fori_loop(0, n_rows, send_row, 0)
     swap(n_rows - 1).start()
+    lax.fori_loop(0, n_rows, own_row, 0)
 
     def finish(i, carry):
         swap(i).wait_recv()
@@ -332,7 +329,7 @@
     dma = pltpu.SemaphoreType.DMA
     edge_len, width = vals.shape[1:]
     slots = cols.shape[2]
-    n_rows, kept = wanted.shape
+    kept, _, n_rows = wanted.shape
     half = kept // 2
     share = (n_rows, edge_len, half * edge_len)
     return pl.pallas_call(
@@ -374,7 +371,7 @@
 
 
 def per_device(p_vals, p_cols, c_cols):
-    return fused(p_vals, p_cols[:, None, :], c_cols[:, 0, :])
+    return fused(p_vals, p_cols[:, None, :], jnp.transpose(c_cols, (2, 1, 0)))
 
 
 def solution(mesh):

time: 87.7 us -> 74.8 us (0.85)
  the two profiles are of different devices: /device:TPU:1 before, /device:TPU:48 now
where the time goes in v5:
time: 74.8 us; the launch traced here: 74.6 us
  Pallas kernels  72.7 us (97%)
  local copies, waits for them, and re-layouts  1.88 us (3%)
    pallas_call x1, Pallas kernels, fused(): pl.pallas_call(fused_kernel, name='gather_pick_multiply_swap', out_shape=...  72.7 us
    unnamed x1, local copies, waits for them, and re-layouts  1.88 us

profile of v5, /device:TPU:48, one launch (start us, length us, event | category | flops | bytes accessed | tf_op | source)
XLA Modules:
  0.0 74.6 jit_solution(16730871526404222457)
XLA Ops:
  0.0 72.7 %gather_pick_multiply_swap.1 = bf16[16,1,64,192]{3,2,1,0:T(8,128)(2,1)} custom-call(bf16[1,64,768]{2,1,0:T(8,128)(2,1)} %vals.1, s32[1,1,12]{2,1,0:T(1,128)} %bitcast.3, s32[6,1,16]{2,1,0:T(1,128)} %bitcast.2), custom_call_target="tpu_custom_call" | custom-call | tf_op jit(solution)/shard_map/gather_pick_multiply_swap/pallas_call | solution.py:335
  72.7 1.9 %copy.5 = bf16[16,1,64,192]{3,2,1,0:T(8,128)(2,1)} copy(bf16[16,1,64,192]{3,2,1,0:T(8,128)(2,1)} %gather_pick_multiply_swap.1) | data formatting | bytes 786432

commit v6 on v5

--- a/solution.py
+++ b/solution.py
@@ -267,36 +267,42 @@
             device_id_type=MESH,
         )
 
-    def one_row(side, into, i):
+    def one_row(side, into, i, buf):
         for o in range(half):
             r = i * kept + side * half + o
             t = target(i, side, o)
             for p in range(slots // 2):
                 first = twice[t, picks[r, 2 * p]]
                 second = twice[t, picks[r, 2 * p + 1]]
-                chosen[side, o * edge_len : (o + 1) * edge_len, p * LANES : (p + 1) * LANES] = jnp.where(
+                chosen[buf, o * edge_len : (o + 1) * edge_len, p * LANES : (p + 1) * LANES] = jnp.where(
                     low, first, second
                 )
         into[i] = lax.dot_general(
-            rowv[i], chosen[side], (((1,), (1,)), ((), ())), preferred_element_type=jnp.float32
+            rowv[i], chosen[buf], (((1,), (1,)), ((), ())), preferred_element_type=jnp.float32
         )
 
-    def send_row(i, carry):
-        one_row(1, send, i)
-
-        @pl.when(i > 0)
+    group = chosen.shape[0]
+
+    def send_rows(g, carry):
+        for k in range(group):
+            one_row(1, send, g * group + k, k)
+
+        @pl.when(g > 0)
         def _():
-            swap(i - 1).start()
-
-        return carry
-
-    def own_row(i, carry):
-        one_row(0, own, i)
-        return carry
-
-    lax.fori_loop(0, n_rows, send_row, 0)
-    swap(n_rows - 1).start()
-    lax.fori_loop(0, n_rows, own_row, 0)
+            for k in range(group):
+                swap((g - 1) * group + k).start()
+
+        return carry
+
+    def own_rows(g, carry):
+        for k in range(group):
+            one_row(0, own, g * group + k, k)
+        return carry
+
+    lax.fori_loop(0, n_rows // group, send_rows, 0)
+    for k in range(group):
+        swap(n_rows - group + k).start()
+    lax.fori_loop(0, n_rows // group, own_rows, 0)
 
     def finish(i, carry):
         swap(i).wait_recv()
@@ -352,7 +358,7 @@
             pltpu.VMEM((n_rows * kept, LANES), jnp.int32),
             pltpu.VMEM((n_rows * kept, LANES), jnp.int32),
             pltpu.SMEM((n_rows * kept, LANES), jnp.int32),
-            pltpu.VMEM((2, half * edge_len, width), vals.dtype),
+            pltpu.VMEM((4, half * edge_len, width), vals.dtype),
             pltpu.VMEM(share, jnp.float32),
             pltpu.VMEM(share, jnp.float32),
             pltpu.VMEM(share, jnp.float32),

time: 74.8 us -> 71.6 us (0.957)
  the two profiles are of different devices: /device:TPU:48 before, /device:TPU:1 now
where the time goes in v6:
time: 71.6 us; the launch traced here: 71.3 us
  Pallas kernels  69.4 us (97%)
  local copies, waits for them, and re-layouts  1.88 us (3%)
    pallas_call x1, Pallas kernels, fused(): pl.pallas_call(fused_kernel, name='gather_pick_multiply_swap', out_shape=...  69.4 us
    unnamed x1, local copies, waits for them, and re-layouts  1.88 us

profile of v6, /device:TPU:1, one launch (start us, length us, event | category | flops | bytes accessed | tf_op | source)
XLA Modules:
  0.0 71.3 jit_solution(13595757216634189461)
XLA Ops:
  0.0 69.4 %gather_pick_multiply_swap.1 = bf16[16,1,64,192]{3,2,1,0:T(8,128)(2,1)} custom-call(bf16[1,64,768]{2,1,0:T(8,128)(2,1)} %vals.1, s32[1,1,12]{2,1,0:T(1,128)} %bitcast.3, s32[6,1,16]{2,1,0:T(1,128)} %bitcast.2), custom_call_target="tpu_custom_call" | custom-call | tf_op jit(solution)/shard_map/gather_pick_multiply_swap/pallas_call | solution.py:341
  69.4 1.9 %copy.5 = bf16[16,1,64,192]{3,2,1,0:T(8,128)(2,1)} copy(bf16[16,1,64,192]{3,2,1,0:T(8,128)(2,1)} %gather_pick_multiply_swap.1) | data formatting | bytes 786432
